TPU v7x, 32 devices: a whole 2x2x4 slice. The times are simulated.
32 devices in a mesh: fsdp: 8 (over z, x), tensor: 4 (over y, core).
Axes of the slice: x: 2, y: 2, z: 4, core: 2. Of those that a mesh axis runs over, the one named last changes fastest.
Arguments:
- inputs: float32 [16384, 768], P(('fsdp', 'tensor')), may hold values from -10 to 10
- qkv_weight: bfloat16 [3, 768, 768], P(None, 'fsdp', 'tensor'), may hold values from -0.21875 to 0.21875
- out_weight: bfloat16 [768, 768], P('tensor', 'fsdp'), may hold values from -0.4375 to 0.4375
- conv_weight: float32 [12, 33], replicated, may hold values from -1 to 1
- up_weight: bfloat16 [768, 3072], P('fsdp', 'tensor'), may hold values from -0.21875 to 0.21875
- down_weight: bfloat16 [3072, 768], P('tensor', 'fsdp'), may hold values from -0.109375 to 0.109375
- mix_gain: float32 [768], replicated, may hold values from 0.25 to 1.75
- mix_bias: float32 [768], replicated, may hold values from -1.2 to 1.2
- feed_gain: float32 [768], replicated, may hold values from 0.25 to 1.75
- feed_bias: float32 [768], replicated, may hold values from -1.2 to 1.2
- out_grad: float32 [16384, 768], P(('fsdp', 'tensor')), may hold values from -6 to 6
Outputs:
- output: float32 [16384, 768], P(('fsdp', 'tensor'))
- input_grad: float32 [16384, 768], P(('fsdp', 'tensor'))
- qkv_grad: float32 [3, 768, 768], P(None, 'fsdp', 'tensor')
- out_weight_grad: float32 [768, 768], P('tensor', 'fsdp')
- conv_grad: float32 [12, 33], replicated
- up_grad: float32 [768, 3072], P('fsdp', 'tensor')
- down_grad: float32 [3072, 768], P('tensor', 'fsdp')
- mix_gain_grad: float32 [768], replicated
- mix_bias_grad: float32 [768], replicated
- feed_gain_grad: float32 [768], replicated
- feed_bias_grad: float32 [768], replicated
All inputs are finite; a program needn't handle non-finite values.
Results may differ from a plain program's by a relative error of at most 0.014.
Values may be sent and summed in bfloat16 or wider, within the bound.
No kernel may reach another device: no remote copies, remote signals or barrier semaphores. Data moves between devices by JAX's collectives and lax.ppermute only.
A program may use at most 192 MiB of HBM per device.

v0:
```python
import jax
import jax.numpy as jnp
from jax import lax
from jax.sharding import PartitionSpec as P

HD = 64
LANDMARKS = 64
ITERS = 6


def in_blocks(value, dim, count):
    lengths = value.shape
    tiles = value.reshape(*lengths[:dim], count, lengths[dim] // count, *lengths[dim + 1 :])
    return jnp.moveaxis(tiles, dim, 0)


def sum_at_owner(value, axis, dim):
    tiles = in_blocks(value, dim, lax.axis_size(axis))
    arrived = lax.all_to_all(tiles, axis, split_axis=0, concat_axis=0, tiled=True)
    return arrived.astype(jnp.float32).sum(axis=0)


def landmarks(query, key):
    heads, length, width = query.shape
    factor = width ** (-0.25)
    scaled_q = query * factor
    scaled_k = key * factor
    marks_q = jnp.mean(scaled_q.reshape(heads, LANDMARKS, length // LANDMARKS, width), axis=2)
    marks_k = jnp.mean(scaled_k.reshape(heads, LANDMARKS, length // LANDMARKS, width), axis=2)
    inner = jnp.einsum("hid,hjd->hij", marks_q, marks_k, precision=lax.Precision.HIGHEST)
    kernel_two = jax.nn.softmax(inner, axis=-1)
    return (scaled_q, scaled_k, marks_q, marks_k, kernel_two)


def column_peak(query, key):
    kernel_two = landmarks(query, key)[4]
    return jnp.max(jnp.sum(kernel_two, axis=1), axis=1)


def mixing(query, key, value, conv, inverse):
    high = lax.Precision.HIGHEST
    scaled_q, scaled_k, marks_q, marks_k, kernel_two = landmarks(query, key)
    length = query.shape[1]
    kernel_one = jax.nn.softmax(
        jnp.einsum("hnd,hjd->hnj", scaled_q, marks_k, precision=high), axis=-1
    )
    kernel_three = jax.nn.softmax(
        jnp.einsum("hid,hnd->hin", marks_q, scaled_k, precision=high), axis=-1
    )
    approx = jnp.swapaxes(kernel_two, 1, 2) * inverse[:, None, None]
    ident = jnp.eye(kernel_two.shape[1], dtype=jnp.float32)
    for step in range(ITERS):
        prod = jnp.einsum("hij,hjk->hik", kernel_two, approx, precision=high)
        inner = 7.0 * ident - prod
        inner = 15.0 * ident - jnp.einsum("hij,hjk->hik", prod, inner, precision=high)
        inner = 13.0 * ident - jnp.einsum("hij,hjk->hik", prod, inner, precision=high)
        approx = jnp.einsum("hij,hjk->hik", 0.25 * approx, inner, precision=high)
    summary = jnp.einsum("hin,hnd->hid", kernel_three, value, precision=high)
    carried = jnp.einsum("hij,hjd->hid", approx, summary, precision=high)
    mixed = jnp.einsum("hnj,hjd->hnd", kernel_one, carried, precision=high)
    margin = conv.shape[1] // 2
    padded = jnp.pad(value, ((0, 0), (margin, margin), (0, 0)))
    for tap in range(conv.shape[1]):
        mixed = mixed + conv[:, tap][:, None, None] * padded[:, tap : tap + length, :]
    return mixed


def gelu_tanh(value):
    return jax.nn.gelu(value, approximate=True)


def norm_forward(rows, gain, shift):
    center = rows - jnp.mean(rows, axis=-1, keepdims=True)
    spread = jnp.mean(center * center, axis=-1, keepdims=True)
    factor = lax.rsqrt(spread + 1e-05)
    normed = center * factor
    return (normed * gain + shift, normed, factor)


def norm_backward(cotan, normed, factor, gain):
    scaled = cotan * gain
    return factor * (
        scaled
        - jnp.mean(scaled, axis=-1, keepdims=True)
        - normed * jnp.mean(scaled * normed, axis=-1, keepdims=True)
    )


def norm_params(cotan, normed):
    return (jnp.sum(cotan * normed, axis=0), jnp.sum(cotan, axis=0))


def shards(
    inputs,
    qkv_weight,
    out_weight,
    conv_weight,
    up_weight,
    down_weight,
    mix_gain,
    mix_bias,
    feed_gain,
    feed_bias,
    out_grad,
):
    place = lax.axis_index("tensor")
    gathered_in = lax.all_gather(inputs.astype(jnp.bfloat16), "tensor", axis=0, tiled=True)
    length = gathered_in.shape[0]
    w_qkv, w_out, w_up, w_down = (
        lax.all_gather(qkv_weight, "fsdp", axis=1, tiled=True),
        lax.all_gather(out_weight, "fsdp", axis=1, tiled=True),
        lax.all_gather(up_weight, "fsdp", axis=0, tiled=True),
        lax.all_gather(down_weight, "fsdp", axis=1, tiled=True),
    )
    columns = w_qkv.shape[2]
    local_heads = columns // HD
    qkv = jnp.einsum("nd,kdc->knc", gathered_in, w_qkv, preferred_element_type=jnp.float32)

    def split_heads(block):
        return block.reshape(length, local_heads, HD).transpose(1, 0, 2)

    query, key, value = (split_heads(qkv[0]), split_heads(qkv[1]), split_heads(qkv[2]))
    conv_local = lax.dynamic_slice_in_dim(conv_weight, place * local_heads, local_heads, 0)
    peak_local = column_peak(query, key)
    peak = lax.pmax(peak_local, "fsdp")
    inverse = 1.0 / peak
    mixed, mixing_back = jax.vjp(mixing, query, key, value, conv_local, inverse)
    context = mixed.transpose(1, 0, 2).reshape(length, columns).astype(jnp.bfloat16)
    attended = lax.psum_scatter(
        jnp.dot(context, w_out, preferred_element_type=jnp.float32),
        "tensor",
        scatter_dimension=0,
        tiled=True,
    )
    mixed_rows, normed_mix, factor_mix = norm_forward(inputs + attended, mix_gain, mix_bias)
    mixed_low = lax.all_gather(mixed_rows.astype(jnp.bfloat16), "tensor", axis=0, tiled=True)
    up_rows = jnp.dot(mixed_low, w_up, preferred_element_type=jnp.float32)
    act, gelu_back = jax.vjp(gelu_tanh, up_rows)
    act_low = act.astype(jnp.bfloat16)
    fed = lax.psum_scatter(
        jnp.dot(act_low, w_down, preferred_element_type=jnp.float32).astype(jnp.bfloat16),
        "tensor",
        scatter_dimension=0,
        tiled=True,
    ).astype(jnp.float32)
    output, normed_feed, factor_feed = norm_forward(mixed_rows + fed, feed_gain, feed_bias)
    grad_feed = norm_backward(out_grad, normed_feed, factor_feed, feed_gain)
    feed_gain_part, feed_bias_part = norm_params(out_grad, normed_feed)
    grad_down = lax.all_gather(grad_feed.astype(jnp.bfloat16), "tensor", axis=0, tiled=True)
    down_grad = jnp.einsum("nf,nd->fd", act_low, grad_down, preferred_element_type=jnp.float32)
    grad_act = jnp.einsum("nd,fd->nf", grad_down, w_down, preferred_element_type=jnp.float32)
    grad_up = gelu_back(grad_act)[0].astype(jnp.bfloat16)
    up_grad = jnp.einsum("nd,nf->df", mixed_low, grad_up, preferred_element_type=jnp.float32)
    grad_mixed_rows = grad_feed + lax.psum_scatter(
        jnp.einsum("nf,df->nd", grad_up, w_up, preferred_element_type=jnp.float32).astype(
            jnp.bfloat16
        ),
        "tensor",
        scatter_dimension=0,
        tiled=True,
    ).astype(jnp.float32)
    grad_mix = norm_backward(grad_mixed_rows, normed_mix, factor_mix, mix_gain)
    mix_gain_part, mix_bias_part = norm_params(grad_mixed_rows, normed_mix)
    grad_attended = lax.all_gather(grad_mix.astype(jnp.bfloat16), "tensor", axis=0, tiled=True)
    out_weight_grad = jnp.einsum(
        "nc,nd->cd", context, grad_attended, preferred_element_type=jnp.float32
    )
    grad_context = jnp.einsum("nd,cd->nc", grad_attended, w_out, preferred_element_type=jnp.float32)
    grad_mixed = grad_context.reshape(length, local_heads, HD).transpose(1, 0, 2)
    grad_query, grad_key, grad_value, grad_conv, grad_inverse = mixing_back(grad_mixed)
    grad_peak = -grad_inverse * inverse * inverse
    head_total = conv_weight.shape[0]
    peak_full = lax.dynamic_update_slice_in_dim(
        jnp.zeros((head_total,), jnp.float32), grad_peak, place * local_heads, 0
    )
    conv_full = lax.dynamic_update_slice_in_dim(
        jnp.zeros(conv_weight.shape, jnp.float32), grad_conv, place * local_heads, 0
    )
    norm_stack = jnp.stack([mix_gain_part, mix_bias_part, feed_gain_part, feed_bias_part])
    peak_sum, conv_grad, norm_sum = lax.psum((peak_full, conv_full, norm_stack), ("fsdp", "tensor"))
    peak_total = lax.dynamic_slice_in_dim(peak_sum, place * local_heads, local_heads, 0)
    owner = jnp.where(peak_local == peak, peak_total, 0.0)
    unused, peak_back = jax.vjp(column_peak, query, key)
    extra_query, extra_key = peak_back(owner)

    def merge_heads(block):
        return block.transpose(1, 0, 2).reshape(length, columns)

    grad_qkv = jnp.stack(
        [
            merge_heads(grad_query + extra_query),
            merge_heads(grad_key + extra_key),
            merge_heads(grad_value),
        ]
    ).astype(jnp.bfloat16)
    qkv_grad = jnp.einsum("nd,knc->kdc", gathered_in, grad_qkv, preferred_element_type=jnp.float32)
    input_grad = grad_mix + lax.psum_scatter(
        jnp.einsum("knc,kdc->nd", grad_qkv, w_qkv, preferred_element_type=jnp.float32).astype(
            jnp.bfloat16
        ),
        "tensor",
        scatter_dimension=0,
        tiled=True,
    ).astype(jnp.float32)
    qkv_share, out_share, up_share, down_share = (
        sum_at_owner(qkv_grad.astype(jnp.bfloat16), "fsdp", 1),
        sum_at_owner(out_weight_grad.astype(jnp.bfloat16), "fsdp", 1),
        sum_at_owner(up_grad.astype(jnp.bfloat16), "fsdp", 0),
        sum_at_owner(down_grad.astype(jnp.bfloat16), "fsdp", 1),
    )
    return (
        output,
        input_grad,
        qkv_share,
        out_share,
        conv_grad,
        up_share,
        down_share,
        norm_sum[0],
        norm_sum[1],
        norm_sum[2],
        norm_sum[3],
    )


def solution(mesh):
    placed = (
        P(("fsdp", "tensor"), None),
        P(None, "fsdp", "tensor"),
        P("tensor", "fsdp"),
        P(),
        P("fsdp", "tensor"),
        P("tensor", "fsdp"),
        P(),
        P(),
        P(),
        P(),
        P(("fsdp", "tensor"), None),
    )
    return jax.shard_map(
        shards,
        mesh=mesh,
        in_specs=placed,
        out_specs=(
            P(("fsdp", "tensor"), None),
            P(("fsdp", "tensor"), None),
            P(None, "fsdp", "tensor"),
            P("tensor", "fsdp"),
            P(),
            P("fsdp", "tensor"),
            P("tensor", "fsdp"),
            P(),
            P(),
            P(),
            P(),
        ),
        check_vma=False,
    )
```

profile of v0, /device:TPU:0, one launch (start us, length us, event | category | flops | bytes accessed | tf_op | source)
XLA Modules:
  0.0 735.5 jit_solution(5595995136005372708)
XLA Ops:
  12.9 35.1 %all_gather.26 = bf16[192,768]{0,1:T(8,128)(2,1)} all-gather(bf16[192,96]{0,1:T(8,128)(2,1)S(1)} %copy.111), channel_id=1, replica_groups=mesh['fsdp'=8,'tensor'=4] {'fsdp'}, dimensions={1}, use_global_device_ids=true | all-gather | bytes 331776 | tf_op jit(solution)/shard_map/all_gather | solution.py:111
  48.0 38.3 %all_gather.24 = bf16[3,768,192]{2,0,1:T(4,128)(2,1)S(1)} all-gather(bf16[3,96,192]{2,0,1:T(4,128)(2,1)S(1)} %copy.100), channel_id=1, replica_groups=mesh['fsdp'=8,'tensor'=4] {'fsdp'}, dimensions={1}, use_global_device_ids=true | all-gather | bytes 995328 | tf_op jit(solution)/shard_map/all_gather | solution.py:110
  87.5 4.6 convolution_bitcast_fusion
  96.3 3.3 copy.103
  99.6 4.4 bitcast_reduce_fusion
  104.0 2.6 fusion.116
  107.3 2.9 fusion.124
  110.2 19.7 %pmax.7 = f32[3]{0:T(128)S(1)} all-reduce(f32[3]{0:T(128)S(1)} %reduce_max.37), channel_id=1, replica_groups=mesh['fsdp'=8,'tensor'=4] {'fsdp'}, use_global_device_ids=true, to_apply=%region_8.0 | all-reduce | flops 3 | bytes 24 | tf_op jit(solution)/shard_map/pmax | solution.py:125
  145.2 14.7 %fusion.56 = bf16[3,2048,64]{1,2,0:T(8,128)(2,1)S(1)} fusion(f32[3,64,64]{2,1,0:T(8,128)S(1)} %fusion.210, f32[3,2048,64]{1,2,0:T(8,128)S(1)} %bitcast.257, f32[3]{0:T(128)S(1)} %copy-done.126, f32[3]{0:T(128)S(1)} %copy-done.138, f32[3]{0:T(128)S(1)} %copy-done.139, f32[3]{0:T(128)S(1)} %copy-done.140, f32[3]{0:T(128)S(1)} %copy-done.141, ...), kind=kOutput, calls=%fused_computation.69 | convolution fusion | flops 328728576 | bytes 4006284 | tf_op jit(solution)/shard_map/jvp(hnj,hjd->hnd)/dot_general | solution.py:60
  160.8 3.7 fusion.211
  165.2 55.7 %reduce-scatter.5.cloned.1.call-done = f32[512,768]{1,0:T(8,128)} async-done(((f32[2048,768]{1,0:T(8,128)}), f32[512,768]{1,0:T(8,128)}) %reduce-scatter.5.cloned.1.call-update) | async-done | bytes 1572880 | tf_op jit(solution)/shard_map/reduce_scatter | solution.py:129
  225.6 27.8 %all-gather.9.cloned.1.call-done = bf16[2048,768]{1,0:T(8,128)(2,1)} async-done(((bf16[512,768]{1,0:T(8,128)(2,1)}), bf16[2048,768]{1,0:T(8,128)(2,1)}) %all-gather.9.cloned.1.call-update) | async-done | bytes 3145744 | tf_op jit(solution)/shard_map/all_gather | solution.py:136
  253.4 7.5 %fusion.212 = f32[2048,768]{1,0:T(8,128)} fusion(bf16[2048,768]{1,0:T(8,128)(2,1)} %all-gather.9.cloned.1.call-done, bf16[768,768]{1,0:T(8,128)(2,1)} %all-gather.11.cloned.1.call-done), kind=kOutput, calls=%fused_computation.447 | convolution fusion | flops 2415919104 | bytes 10616832 | tf_op jit(solution)/shard_map/dot_general | solution.py:137
  260.9 36.0 %all-gather.13.cloned.1.call-done = bf16[768,768]{0,1:T(8,128)(2,1)} async-done(((bf16[768,96]{0,1:T(8,128)(2,1)}), bf16[768,768]{0,1:T(8,128)(2,1)}) %all-gather.13.cloned.1.call-update) | async-done | bytes 1179664 | tf_op jit(solution)/shard_map/all_gather | solution.py:113
  296.9 8.6 %convolution_convert_fusion.1 = bf16[2048,768]{1,0:T(8,128)(2,1)} fusion(bf16[768,768]{0,1:T(8,128)(2,1)} %all-gather.13.cloned.1.call-done, f32[2048,768]{1,0:T(8,128)} %fusion.212), kind=kOutput, calls=%fused_computation.15 | convolution fusion | flops 2431647744 | bytes 10616832 | tf_op jit(solution)/shard_map/dot_general | solution.py:141
  305.6 36.1 %reduce-scatter.7.cloned.1.call-done = bf16[512,768]{1,0:T(8,128)(2,1)} async-done(((bf16[2048,768]{1,0:T(8,128)(2,1)}), bf16[512,768]{1,0:T(8,128)(2,1)}) %reduce-scatter.7.cloned.1.call-update) | async-done | bytes 786448 | tf_op jit(solution)/shard_map/reduce_scatter | solution.py:140
  348.3 28.4 %all-gather.15.cloned.1.call-done = bf16[2048,768]{1,0:T(8,128)(2,1)} async-done(((bf16[512,768]{1,0:T(8,128)(2,1)}), bf16[2048,768]{1,0:T(8,128)(2,1)}) %all-gather.15.cloned.1.call-update) | async-done | bytes 3145744 | tf_op jit(solution)/shard_map/all_gather | solution.py:149
  376.7 8.5 %fusion.9 = bf16[2048,768]{1,0:T(8,128)(2,1)S(1)} fusion(f32[2048,768]{1,0:T(8,128)} %fusion.212, bf16[2048,768]{1,0:T(8,128)(2,1)} %all-gather.15.cloned.1.call-done, bf16[768,768]{0,1:T(8,128)(2,1)} %all-gather.13.cloned.1.call-done), kind=kOutput, calls=%fused_computation.11 | convolution fusion | flops 2447376384 | bytes 13762560 | tf_op jit(solution)/shard_map/nd,fd->nf/dot_general | solution.py:151
  386.9 4.0 convolution_convert_fusion
  391.0 38.0 %reduce-scatter.9.cloned.1.call-done = bf16[512,768]{1,0:T(8,128)(2,1)} async-done(((bf16[2048,768]{1,0:T(8,128)(2,1)}), bf16[512,768]{1,0:T(8,128)(2,1)}) %reduce-scatter.9.cloned.1.call-update) | async-done | bytes 786448 | tf_op jit(solution)/shard_map/reduce_scatter | solution.py:154
  429.0 3.1 multiply_reduce_fusion.1
  436.8 8.0 %convolution_convert_fusion.2 = bf16[768,768]{0,1:T(8,128)(2,1)} fusion(bf16[2048,768]{1,0:T(8,128)(2,1)} %all-gather.15.cloned.1.call-done, f32[2048,768]{1,0:T(8,128)} %fusion.212), kind=kOutput, calls=%fused_computation.133 | convolution fusion | flops 2430664704 | bytes 10616832 | tf_op jit(solution)/shard_map/nf,nd->fd/dot_general | solution.py:150
  444.7 5.5 all-to-all-start.3
  450.4 12.3 %all-gather.17.cloned.1.call-done = bf16[2048,768]{1,0:T(8,128)(2,1)} async-done(((bf16[512,768]{1,0:T(8,128)(2,1)}), bf16[2048,768]{1,0:T(8,128)(2,1)}) %all-gather.17.cloned.1.call-update) | async-done | bytes 3145744 | tf_op jit(solution)/shard_map/all_gather | solution.py:164
  462.7 3.1 fusion.213
  465.8 8.2 %multiply_reduce_fusion.34 = (f32[3]{0:T(128)S(1)}, f32[3]{0:T(128)S(1)}, f32[3]{0:T(128)S(1)}, f32[3]{0:T(128)S(1)}, f32[3]{0:T(128)S(1)}, /*index=5*/f32[3]{0:...) fusion(f32[3,2048,64]{1,2,0:T(8,128)S(1)} %bitcast.250, ...), kind=kLoop, calls=%fused_computation.117 | loop fusion | flops 14155722 | bytes 3145944 | tf_op jit(solution)/shard_map/transpose(jvp())/reduce_sum | solution.py:64
  489.6 7.8 %multiply_reduce_fusion.33 = (f32[3]{0:T(128)S(1)}, f32[3]{0:T(128)S(1)}, f32[3]{0:T(128)S(1)}, f32[3]{0:T(128)S(1)}, f32[3]{0:T(128)S(1)}, /*index=5*/f32[3]{0:...) fusion(f32[3,2048,64]{1,2,0:T(8,128)S(1)} %bitcast.252, ...), kind=kLoop, calls=%fused_computation.116 | loop fusion | flops 12976083 | bytes 7864536 | tf_op jit(solution)/shard_map/transpose(jvp())/reduce_sum | solution.py:64
  504.5 40.0 %all-reduce.67 = (f32[12]{0:T(128)S(1)}, f32[12,33]{1,0:T(8,128)}, f32[4,768]{1,0:T(4,128)}) all-reduce(f32[12]{0:T(128)S(1)} %fusion.168, f32[12,33]{1,0:T(8,128)S(1)} %dynamic_update_slice.7, f32[4,768]{1,0:T(4,128)S(1)} %pad_maximum_fusion.3), channel_id=1, replica_groups=mesh['fsdp'=8,'tensor'=4] {'fsdp','tensor'}, use_global_device_ids=true, to_apply=%region_26.27 | all-reduce | flops 3480 | bytes 27840 | tf_op jit(solution)/shard_map/psum | solution.py:180
  549.8 7.4 %broadcast_multiply_fusion.1 = (f32[3,2048,64]{1,2,0:T(8,128)}, f32[3,2048,64]{1,2,0:T(8,128)}, f32[3,2048,64]{1,2,0:T(8,128)}, f32[3,2048,64]{1,2,0:T(8,128)}, ...) fusion(f32[3,2048,64]{1,2,0:T(8,128)S(1)} %bitcast.253, ...), kind=kLoop, calls=%fused_computation.216 | loop fusion | flops 4718592 | bytes 20447376 | tf_op jit(solution)/shard_map/transpose(jvp())/mul | solution.py:64
  557.4 11.1 %broadcast_multiply_fusion = (f32[3,2048,64]{1,2,0:T(8,128)}, f32[3,2048,64]{1,2,0:T(8,128)}, f32[3,2048,64]{1,2,0:T(8,128)}, f32[3,2048,64]{1,2,0:T(8,128)}, f3...) fusion(f32[3,2048,64]{1,2,0:T(8,128)S(1)} %bitcast.254, ...), kind=kLoop, calls=%fused_computation.215 | loop fusion | flops 7077888 | bytes 29884632 | tf_op jit(solution)/shard_map/transpose(jvp())/mul | solution.py:64
  578.3 3.4 copy.136
  583.7 3.2 copy.139
  588.7 3.3 copy.134
  593.9 3.3 copy.138
  597.2 5.2 fusion.54
  602.5 2.9 fusion.55
  605.5 18.7 %pad_add_fusion = f32[3,2080,64]{1,2,0:T(8,128)S(1)} fusion(f32[3,2048,64]{1,2,0:T(8,128)S(1)} %copy-done.10, f32[3,2048,64]{1,2,0:T(8,128)S(1)} %copy-done.11, f32[3,2048,64]{1,2,0:T(8,128)S(1)} %copy-done.12, f32[3,2048,64]{1,2,0:T(8,128)} %get-tuple-element.129, f32[3,2048,64]{1,2,0:T(8,128)} %get-tuple-element.130, ...), kind=kLoop, calls=%fused_computation.74 | loop fusion | flops 10383360 | bytes 44064768 | tf_op jit(solution)/shard_map/transpose(jvp())/add_any | solution.py:64
  624.2 7.5 %fusion.53 = bf16[3,2048,64]{1,2,0:T(8,128)(2,1)S(1)} fusion(f32[3,64,64]{2,1,0:T(8,128)S(1)} %copy-done.52, f32[3,2048,64]{1,2,0:T(8,128)} %get-tuple-element.119, f32[3,2048,64]{1,2,0:T(8,128)} %get-tuple-element.120, f32[3,2048,64]{1,2,0:T(8,128)} %get-tuple-element.121, f32[3,2048,64]{1,2,0:T(8,128)} %get-tuple-element.123, ...), kind=kOutput, calls=%fused_computation.66 | convolution fusion | flops 305528832 | bytes 13419264 | tf_op jit(solution)/shard_map/transpose(jvp(hin,hnd->hid))/dot_general | solution.py:58
  632.6 4.2 bitcast_convert_fusion
  636.8 6.5 convolution_convert_fusion.3
  643.3 5.4 all-to-all-start.2
  648.7 2.7 convolution_convert_fusion.4
  652.7 24.3 %all-to-all-done.2 = bf16[8,96,768]{2,1,0:T(8,128)(2,1)S(1)} async-done(((bf16[8,96,768]{2,1,0:T(8,128)(2,1)}), bf16[8,96,768]{2,1,0:T(8,128)(2,1)S(1)}, u32[]{:S(2)}, u32[]{:S(2)}) %all-to-all-start.2) | async-done | bytes 1179680 | tf_op jit(solution)/shard_map/all_to_all | solution.py:19
  677.0 3.5 all-to-all-start.1
  680.5 5.0 fusion.61
  689.2 3.1 all-to-all-done.1
  692.4 3.6 all-to-all-start
  700.4 24.3 %all-to-all-done = bf16[8,3,96,192]{2,3,1,0:T(8,128)(2,1)S(1)} async-done(((bf16[8,3,96,192]{2,3,1,0:T(8,128)(2,1)}), bf16[8,3,96,192]{2,3,1,0:T(8,128)(2,1)S(1)}, u32[]{:S(2)}, u32[]{:S(2)}) %all-to-all-start) | async-done | bytes 884768 | tf_op jit(solution)/shard_map/all_to_all | solution.py:19
  (506 shorter events, 100.2 us)
Async XLA Ops:
  8.0 78.3 %all-gather.7.cloned.1.call-start = ((), (), s32[]{:S(2)}) async-start(), calls=%async_computation.8 | async-start | bytes 3932160 | tf_op jit(solution)/shard_map/all_gather | solution.py:107
  10.5 210.4 %reduce-scatter.5.cloned.1.call-start = ((), (), s32[]{:S(2)}) async-start(), calls=%async_computation.9 | async-start | bytes 7864320 | tf_op jit(solution)/shard_map/reduce_scatter | solution.py:129
  11.8 133.1 %copy-start.102 = (f32[3]{0:T(128)}, f32[3]{0:T(128)S(1)}, u32[]{:S(2)}) copy-start(f32[3]{0:T(128)S(1)} %get-tuple-element.89) | copy-start | bytes 40
  11.8 133.1 %copy-start.104 = (f32[3]{0:T(128)}, f32[3]{0:T(128)S(1)}, u32[]{:S(2)}) copy-start(f32[3]{0:T(128)S(1)} %get-tuple-element.90) | copy-start | bytes 40
  93.9 10.0 %copy-start.2 = (f32[1,2048,192]{1,2,0:T(8,128)}, f32[1,2048,192]{1,2,0:T(8,128)S(1)}, u32[]{:S(2)}) copy-start(f32[1,2048,192]{1,2,0:T(8,128)S(1)} %get-tuple-element.116) | copy-start | bytes 4718596
  139.9 296.2 %copy-start.91 = (f32[3,64]{1,0:T(4,128)}, f32[3,64]{1,0:T(4,128)S(1)}, u32[]{:S(2)}) copy-start(f32[3,64]{1,0:T(4,128)S(1)} %get-tuple-element.154) | copy-start | bytes 2308
  144.5 15.4 %copy-start.85 = (f32[3,64,64]{2,1,0:T(8,128)}, f32[3,64,64]{2,1,0:T(8,128)S(1)}, u32[]{:S(2)}) copy-start(f32[3,64,64]{2,1,0:T(8,128)S(1)} %fusion.210) | copy-start | bytes 147460
  145.2 15.6 %copy-start.22 = (bf16[192,768]{0,1:T(8,128)(2,1)S(1)}, bf16[192,768]{0,1:T(8,128)(2,1)}, u32[]{:S(2)}) copy-start(bf16[192,768]{0,1:T(8,128)(2,1)} %all_gather.26) | copy-start | bytes 884740
  164.6 61.0 %all-gather.11.cloned.1.call-start = ((), (), s32[]{:S(2)}) async-start(), calls=%async_computation.11 | async-start | bytes 1327104 | tf_op jit(solution)/shard_map/all_gather | solution.py:112
  165.1 88.3 %all-gather.9.cloned.1.call-start = ((), (), s32[]{:S(2)}) async-start(), calls=%async_computation.10 | async-start | bytes 3932160 | tf_op jit(solution)/shard_map/all_gather | solution.py:136
  224.9 72.0 %all-gather.13.cloned.1.call-start = ((), (), s32[]{:S(2)}) async-start(), calls=%async_computation.12 | async-start | bytes 1327104 | tf_op jit(solution)/shard_map/all_gather | solution.py:113
  225.5 116.2 %reduce-scatter.7.cloned.1.call-start = ((), (), s32[]{:S(2)}) async-start(), calls=%async_computation.13 | async-start | bytes 3932160 | tf_op jit(solution)/shard_map/reduce_scatter | solution.py:140
  305.5 71.2 %all-gather.15.cloned.1.call-start = ((), (), s32[]{:S(2)}) async-start(), calls=%async_computation.14 | async-start | bytes 3932160 | tf_op jit(solution)/shard_map/all_gather | solution.py:149
  348.2 80.8 %reduce-scatter.9.cloned.1.call-start = ((), (), s32[]{:S(2)}) async-start(), calls=%async_computation.15 | async-start | bytes 3932160 | tf_op jit(solution)/shard_map/reduce_scatter | solution.py:154
  376.7 10.2 %copy-start.157 = (bf16[768,768]{1,0:T(8,128)(2,1)S(1)}, bf16[768,768]{1,0:T(8,128)(2,1)}, u32[]{:S(2)}) copy-start(bf16[768,768]{1,0:T(8,128)(2,1)} %all-gather.11.cloned.1.call-done) | copy-start | bytes 3538948
  390.9 71.8 %all-gather.17.cloned.1.call-start = ((), (), s32[]{:S(2)}) async-start(), calls=%async_computation.16 | async-start | bytes 3932160 | tf_op jit(solution)/shard_map/all_gather | solution.py:164
  444.7 198.6 %all-to-all-start.3 = ((bf16[8,768,96]{1,2,0:T(8,128)(2,1)}), bf16[8,768,96]{1,2,0:T(8,128)(2,1)}, u32[]{:S(2)}, u32[]{:S(2)}) async-start(bf16[8,768,96]{1,2,0:T(8,128)(2,1)} %bitcast.70), calls=%async_computation.7 | async-start | bytes 2359296 | tf_op jit(solution)/shard_map/all_to_all | solution.py:19
  450.3 275.5 %reduce-scatter.11.cloned.1.call-start = ((), (), s32[]{:S(2)}) async-start(), calls=%async_computation.17 | async-start | bytes 3932160 | tf_op jit(solution)/shard_map/reduce_scatter | solution.py:197
  465.8 8.2 %copy-start.15 = (f32[3,2048,64]{1,2,0:T(8,128)S(1)}, f32[3,2048,64]{1,2,0:T(8,128)}, u32[]{:S(2)}) copy-start(f32[3,2048,64]{1,2,0:T(8,128)} %copy-done.14) | copy-start | bytes 4718596
  498.3 49.1 %copy-start.35 = (f32[3,64,64]{2,1,0:T(8,128)S(1)}, f32[3,64,64]{2,1,0:T(8,128)}, u32[]{:S(2)}) copy-start(f32[3,64,64]{2,1,0:T(8,128)} %copy-done.34) | copy-start | bytes 147460
  504.5 65.8 %copy-start.51 = (f32[3,64,64]{2,1,0:T(8,128)}, f32[3,64,64]{2,1,0:T(8,128)S(1)}, u32[]{:S(2)}) copy-start(f32[3,64,64]{2,1,0:T(8,128)S(1)} %fusion.214) | copy-start | bytes 147460
  549.6 7.6 %copy-start.103 = (f32[3]{0:T(128)S(1)}, f32[3]{0:T(128)}, u32[]{:S(2)}) copy-start(f32[3]{0:T(128)} %copy-done.102) | copy-start | bytes 40
  549.7 7.6 %copy-start.105 = (f32[3]{0:T(128)S(1)}, f32[3]{0:T(128)}, u32[]{:S(2)}) copy-start(f32[3]{0:T(128)} %copy-done.104) | copy-start | bytes 40
  549.7 7.6 %copy-start.107 = (f32[3]{0:T(128)S(1)}, f32[3]{0:T(128)}, u32[]{:S(2)}) copy-start(f32[3]{0:T(128)} %get-tuple-element.91) | copy-start | bytes 40
  549.7 7.6 %copy-start.109 = (f32[3]{0:T(128)S(1)}, f32[3]{0:T(128)}, u32[]{:S(2)}) copy-start(f32[3]{0:T(128)} %get-tuple-element.92) | copy-start | bytes 40
  549.7 7.6 %copy-start.111 = (f32[3]{0:T(128)S(1)}, f32[3]{0:T(128)}, u32[]{:S(2)}) copy-start(f32[3]{0:T(128)} %get-tuple-element.93) | copy-start | bytes 40
  549.7 7.6 %copy-start.113 = (f32[3]{0:T(128)S(1)}, f32[3]{0:T(128)}, u32[]{:S(2)}) copy-start(f32[3]{0:T(128)} %get-tuple-element.94) | copy-start | bytes 40
  549.7 7.6 %copy-start.115 = (f32[3]{0:T(128)S(1)}, f32[3]{0:T(128)}, u32[]{:S(2)}) copy-start(f32[3]{0:T(128)} %get-tuple-element.95) | copy-start | bytes 40
  549.7 7.6 %copy-start.117 = (f32[3]{0:T(128)S(1)}, f32[3]{0:T(128)}, u32[]{:S(2)}) copy-start(f32[3]{0:T(128)} %get-tuple-element.96) | copy-start | bytes 40
  549.7 7.6 %copy-start.119 = (f32[3]{0:T(128)S(1)}, f32[3]{0:T(128)}, u32[]{:S(2)}) copy-start(f32[3]{0:T(128)} %get-tuple-element.97) | copy-start | bytes 40
  549.7 7.6 %copy-start.121 = (f32[3]{0:T(128)S(1)}, f32[3]{0:T(128)}, u32[]{:S(2)}) copy-start(f32[3]{0:T(128)} %get-tuple-element.98) | copy-start | bytes 40
  549.7 7.6 %copy-start.123 = (f32[3]{0:T(128)S(1)}, f32[3]{0:T(128)}, u32[]{:S(2)}) copy-start(f32[3]{0:T(128)} %get-tuple-element.99) | copy-start | bytes 40
  549.8 7.6 %copy-start.125 = (f32[3]{0:T(128)S(1)}, f32[3]{0:T(128)}, u32[]{:S(2)}) copy-start(f32[3]{0:T(128)} %get-tuple-element.100) | copy-start | bytes 40
  549.8 7.6 %copy-start.127 = (f32[3]{0:T(128)S(1)}, f32[3]{0:T(128)}, u32[]{:S(2)}) copy-start(f32[3]{0:T(128)} %get-tuple-element.70) | copy-start | bytes 40
  549.8 7.6 %copy-start.129 = (f32[3]{0:T(128)S(1)}, f32[3]{0:T(128)}, u32[]{:S(2)}) copy-start(f32[3]{0:T(128)} %get-tuple-element.83) | copy-start | bytes 40
  549.8 7.6 %copy-start.131 = (f32[3]{0:T(128)S(1)}, f32[3]{0:T(128)}, u32[]{:S(2)}) copy-start(f32[3]{0:T(128)} %get-tuple-element.84) | copy-start | bytes 40
  557.4 11.2 %copy-start.16 = (f32[3,2048,64]{1,2,0:T(8,128)S(1)}, f32[3,2048,64]{1,2,0:T(8,128)}, u32[]{:S(2)}) copy-start(f32[3,2048,64]{1,2,0:T(8,128)} %copy-done.14) | copy-start | bytes 4718596
  557.4 11.2 %copy-start.86 = (f32[3,64,64]{2,1,0:T(8,128)S(1)}, f32[3,64,64]{2,1,0:T(8,128)}, u32[]{:S(2)}) copy-start(f32[3,64,64]{2,1,0:T(8,128)} %copy-done.85) | copy-start | bytes 147460
  605.5 18.7 %copy-start.52 = (f32[3,64,64]{2,1,0:T(8,128)S(1)}, f32[3,64,64]{2,1,0:T(8,128)}, u32[]{:S(2)}) copy-start(f32[3,64,64]{2,1,0:T(8,128)} %copy-done.51) | copy-start | bytes 147460
  624.2 8.4 %copy-start.33 = (bf16[3,768,192]{2,0,1:T(4,128)(2,1)S(1)}, bf16[3,768,192]{2,0,1:T(4,128)(2,1)}, u32[]{:S(2)}) copy-start(bf16[3,768,192]{2,0,1:T(4,128)(2,1)} %copy-done.32) | copy-start | bytes 2654212
  624.2 8.4 %copy-start.158 = (bf16[3,2048,64]{1,2,0:T(8,128)(2,1)S(1)}, bf16[3,2048,64]{1,2,0:T(8,128)(2,1)}, u32[]{:S(2)}) copy-start(bf16[3,2048,64]{1,2,0:T(8,128)(2,1)} %fusion.54) | copy-start | bytes 2359300
  624.2 8.4 %copy-start.160 = (bf16[3,2048,64]{1,2,0:T(8,128)(2,1)S(1)}, bf16[3,2048,64]{1,2,0:T(8,128)(2,1)}, u32[]{:S(2)}) copy-start(bf16[3,2048,64]{1,2,0:T(8,128)(2,1)} %fusion.55) | copy-start | bytes 2359300
  643.3 33.7 %all-to-all-start.2 = ((bf16[8,96,768]{2,1,0:T(8,128)(2,1)}), bf16[8,96,768]{2,1,0:T(8,128)(2,1)S(1)}, u32[]{:S(2)}, u32[]{:S(2)}) async-start(bf16[8,96,768]{2,1,0:T(8,128)(2,1)} %bitcast.273), calls=%async_computation.6 | async-start | bytes 2359296 | tf_op jit(solution)/shard_map/all_to_all | solution.py:19
  651.4 29.1 %copy-start.79 = (bf16[3,2048,64]{1,2,0:T(8,128)(2,1)S(1)}, bf16[3,2048,64]{1,2,0:T(8,128)(2,1)}, u32[]{:S(2)}) copy-start(bf16[3,2048,64]{1,2,0:T(8,128)(2,1)} %copy-done.78) | copy-start | bytes 2359300
  651.8 28.7 %copy-start.159 = (bf16[3,2048,64]{1,2,0:T(8,128)(2,1)S(1)}, bf16[3,2048,64]{1,2,0:T(8,128)(2,1)}, u32[]{:S(2)}) copy-start(bf16[3,2048,64]{1,2,0:T(8,128)(2,1)} %fusion.54) | copy-start | bytes 2359300
  677.0 15.4 %all-to-all-start.1 = ((bf16[8,192,96]{2,1,0:T(8,128)(2,1)}), bf16[8,192,96]{2,1,0:T(8,128)(2,1)S(1)}, u32[]{:S(2)}, u32[]{:S(2)}) async-start(bf16[8,192,96]{2,1,0:T(8,128)(2,1)} %bitcast.249), calls=%async_computation.5 | async-start | bytes 786432 | tf_op jit(solution)/shard_map/all_to_all | solution.py:19
  692.4 32.3 %all-to-all-start = ((bf16[8,3,96,192]{2,3,1,0:T(8,128)(2,1)}), bf16[8,3,96,192]{2,3,1,0:T(8,128)(2,1)S(1)}, u32[]{:S(2)}, u32[]{:S(2)}) async-start(bf16[8,3,96,192]{2,3,1,0:T(8,128)(2,1)} %bitcast.248), calls=%async_computation.4 | async-start | bytes 2359296 | tf_op jit(solution)/shard_map/all_to_all | solution.py:19
  699.0 26.8 %copy-start.19 = (f32[512,768]{1,0:T(8,128)S(1)}, f32[512,768]{1,0:T(8,128)}, u32[]{:S(2)}) copy-start(f32[512,768]{1,0:T(8,128)} %get-tuple-element.108) | copy-start | bytes 4718596
  (130 other events, 342.1 us)
Sparse Core Ops, SparseCore 0:
  11.0 31.2 all-gather.6
  164.7 56.1 reduce-scatter.4
  391.0 37.8 reduce-scatter.8
  636.9 38.9 reduce-scatter.10
Sparse Core Ops, SparseCore 1:
  167.2 38.7 all-gather.10
  225.0 28.3 all-gather.8
  255.5 41.4 all-gather.12
  305.6 36.1 reduce-scatter.6
  348.3 28.3 all-gather.14
  434.3 28.3 all-gather.16
where the time goes:
time: 744 us; the launch traced here: 736 us
  waiting for transfers between devices  287 us (39%)
  matrix products  143 us (19%)
  blocking collectives  133 us (18%)
  other arithmetic  90.6 us (12%)
  local copies, waits for them, and re-layouts  45 us (6%)
  starting transfers between devices  18.5 us (2%)
  between operations  18.4 us (2%)
    reduce_scatter x1, waiting for transfers between devices, shards(): lax.psum_scatter(jnp.dot(context, w_out, preferred_element_type=jnp.float...  55.7 us
    all_to_all x4, waiting for transfers between devices, sum_at_owner(): lax.all_to_all(tiles, axis, split_axis=0, concat_axis=0, tiled=True)  51.7 us
    psum x1, blocking collectives, shards(): lax.psum((peak_full, conv_full, norm_stack), ('fsdp', 'tensor'))  40 us
    all_gather x1, blocking collectives, shards(): lax.all_gather(qkv_weight, 'fsdp', axis=1, tiled=True)  38.3 us
    reduce_scatter x1, waiting for transfers between devices, shards(): lax.psum_scatter(jnp.einsum('nf,df->nd', grad_up, w_up, preferred_element...  38 us
    reduce_scatter x1, waiting for transfers between devices, shards(): lax.psum_scatter(jnp.dot(act_low, w_down, preferred_element_type=jnp.floa...  36.1 us
    all_gather x1, waiting for transfers between devices, shards(): lax.all_gather(down_weight, 'fsdp', axis=1, tiled=True)  36 us
    all_gather x1, blocking collectives, shards(): lax.all_gather(out_weight, 'fsdp', axis=1, tiled=True)  35.1 us
  transfers between devices with their start and end apart: 14, of which 10 were waited for; matrix products, arithmetic and copies ran while one was open for 24% of the time, Pallas kernels for 0%

commit v1 on v0

--- a/solution.py
+++ b/solution.py
@@ -106,11 +106,24 @@
     place = lax.axis_index("tensor")
     gathered_in = lax.all_gather(inputs.astype(jnp.bfloat16), "tensor", axis=0, tiled=True)
     length = gathered_in.shape[0]
+
+    def save_core(bus_axis, sheet):
+        axis_len = lax.axis_size(bus_axis)
+        xs_all = [(c, (c + 1) % axis_len) for c in range(axis_len)]
+        row_list = [(c, (c - 1) % axis_len) for c in range(axis_len)]
+        y_new, b_next = ([sheet], [sheet])
+        for _ in range(axis_len // 2):
+            y_new.append(lax.ppermute(y_new[-1], axis_name=bus_axis, perm=xs_all))
+        for _ in range((axis_len - 1) // 2):
+            b_next.append(lax.ppermute(b_next[-1], axis_name=bus_axis, perm=row_list))
+        kept_arr = jnp.concatenate([*y_new[::-1], *b_next[1:]], 1)
+        return jnp.roll(kept_arr, (lax.axis_index(bus_axis) - axis_len // 2) * sheet.shape[1], 1)
+
     w_qkv, w_out, w_up, w_down = (
         lax.all_gather(qkv_weight, "fsdp", axis=1, tiled=True),
         lax.all_gather(out_weight, "fsdp", axis=1, tiled=True),
         lax.all_gather(up_weight, "fsdp", axis=0, tiled=True),
-        lax.all_gather(down_weight, "fsdp", axis=1, tiled=True),
+        save_core("fsdp", down_weight),
     )
     columns = w_qkv.shape[2]
     local_heads = columns // HD

time: 744 us -> 721 us (0.969)
  waiting for transfers between devices: 287 us -> 236 us
  starting transfers between devices: 18.5 us -> 34.2 us
  local copies, waits for them, and re-layouts: 45 us -> 57.9 us
    all_gather x1 -> x0, waiting for transfers between devices: 36 us -> none  [shards(): lax.all_gather(down_weight, 'fsdp', axis=1, tiled=True)]
    all_gather x1, waiting for transfers between devices: 27.8 us -> 0.01 us  [shards(): lax.all_gather(mixed_rows.astype(jnp.bfloat16), 'tensor', axis=0, tiled=T...]
    unnamed x331 -> x356, local copies, waits for them, and re-layouts: 10.9 us -> 34.4 us
    ppermute x0 -> x7, waiting for transfers between devices: none -> 16.5 us  [the longest x4 16.5 us: save_core(): y_new.append(lax.ppermute(y_new[-1], axis_name=bus_axis, perm=xs_all))]
    ppermute x0 -> x7, starting transfers between devices: none -> 15.9 us  [the longest x3 14.3 us: save_core(): b_next.append(lax.ppermute(b_next[-1], axis_name=bus_axis, perm=row_list))]
  transfers between devices with their start and end apart: 14 -> 20, of which waited for: 10 -> 12; matrix products, arithmetic and copies ran while one was open for 24% -> 26% of each run, Pallas kernels for 0% -> 0%
where the time goes in v1:
time: 721 us; the launch traced here: 712 us
  waiting for transfers between devices  236 us (33%)
  matrix products  139 us (19%)
  blocking collectives  134 us (19%)
  other arithmetic  92.5 us (13%)
  local copies, waits for them, and re-layouts  57.9 us (8%)
  starting transfers between devices  34.2 us (5%)
  between operations  18.5 us (3%)
    reduce_scatter x1, waiting for transfers between devices, shards(): lax.psum_scatter(jnp.dot(context, w_out, preferred_element_type=jnp.float...  55.7 us
    all_to_all x4, waiting for transfers between devices, sum_at_owner(): lax.all_to_all(tiles, axis, split_axis=0, concat_axis=0, tiled=True)  53.1 us
    psum x1, blocking collectives, shards(): lax.psum((peak_full, conv_full, norm_stack), ('fsdp', 'tensor'))  40.4 us
    all_gather x1, blocking collectives, shards(): lax.all_gather(qkv_weight, 'fsdp', axis=1, tiled=True)  38.3 us
    reduce_scatter x1, waiting for transfers between devices, shards(): lax.psum_scatter(jnp.einsum('nf,df->nd', grad_up, w_up, preferred_element...  38 us
    all_gather x1, blocking collectives, shards(): lax.all_gather(out_weight, 'fsdp', axis=1, tiled=True)  35.1 us
    unnamed x356, local copies, waits for them, and re-layouts  34.4 us
    reduce_scatter x1, waiting for transfers between devices, shards(): lax.psum_scatter(jnp.dot(act_low, w_down, preferred_element_type=jnp.floa...  34 us
  transfers between devices with their start and end apart: 20, of which 12 were waited for; matrix products, arithmetic and copies ran while one was open for 26% of the time, Pallas kernels for 0%

profile of v1, /device:TPU:0, one launch (start us, length us, event | category | flops | bytes accessed | tf_op | source)
XLA Modules:
  0.0 712.4 jit_solution(12458702161979041531)
XLA Ops:
  12.9 35.1 %all_gather.23 = bf16[192,768]{0,1:T(8,128)(2,1)} all-gather(bf16[192,96]{0,1:T(8,128)(2,1)S(1)} %copy.111), channel_id=1, replica_groups=mesh['fsdp'=8,'tensor'=4] {'fsdp'}, dimensions={1}, use_global_device_ids=true | all-gather | bytes 331776 | tf_op jit(solution)/shard_map/all_gather | solution.py:124
  48.0 38.3 %all_gather.21 = bf16[3,768,192]{2,0,1:T(4,128)(2,1)S(1)} all-gather(bf16[3,96,192]{2,0,1:T(4,128)(2,1)S(1)} %copy.100), channel_id=1, replica_groups=mesh['fsdp'=8,'tensor'=4] {'fsdp'}, dimensions={1}, use_global_device_ids=true | all-gather | bytes 995328 | tf_op jit(solution)/shard_map/all_gather | solution.py:123
  87.6 4.6 convolution_bitcast_fusion
  96.2 3.3 copy.103
  99.5 4.4 bitcast_reduce_fusion
  107.2 2.9 fusion.129
  110.2 19.9 %pmax.7 = f32[3]{0:T(128)S(1)} all-reduce(f32[3]{0:T(128)S(1)} %reduce_max.37), channel_id=1, replica_groups=mesh['fsdp'=8,'tensor'=4] {'fsdp'}, use_global_device_ids=true, to_apply=%region_8.9 | all-reduce | flops 3 | bytes 24 | tf_op jit(solution)/shard_map/pmax | solution.py:138
  145.8 14.4 %fusion.56 = bf16[3,2048,64]{1,2,0:T(8,128)(2,1)S(1)} fusion(f32[3,64,64]{2,1,0:T(8,128)S(1)} %fusion.217, f32[3,2048,64]{1,2,0:T(8,128)S(1)} %bitcast.255, f32[3]{0:T(128)S(1)} %copy-done.131, f32[3]{0:T(128)S(1)} %copy-done.143, f32[3]{0:T(128)S(1)} %copy-done.144, f32[3]{0:T(128)S(1)} %copy-done.145, f32[3]{0:T(128)S(1)} %copy-done.146, ...), kind=kOutput, calls=%fused_computation.69 | convolution fusion | flops 328728576 | bytes 4006284 | tf_op jit(solution)/shard_map/jvp(hnj,hjd->hnd)/dot_general | solution.py:60
  160.2 3.7 fusion.218
  164.6 55.7 %reduce-scatter.5.cloned.1.call-done = f32[512,768]{1,0:T(8,128)} async-done(((f32[2048,768]{1,0:T(8,128)}), f32[512,768]{1,0:T(8,128)}) %reduce-scatter.5.cloned.1.call-update) | async-done | bytes 1572880 | tf_op jit(solution)/shard_map/reduce_scatter | solution.py:142
  225.8 6.9 collective-permute-done
  233.4 4.7 collective-permute-start.4
  238.1 3.2 collective-permute-done.1
  242.1 4.6 collective-permute-start.5
  246.7 3.3 collective-permute-done.2
  250.0 5.0 collective-permute-start.6
  254.9 3.2 collective-permute-done.3
  278.9 4.8 fusion.219
  283.8 2.7 copy-done.168
  286.4 6.7 convolution_convert_fusion.1
  293.1 34.0 %reduce-scatter.7.cloned.1.call-done = bf16[512,768]{1,0:T(8,128)(2,1)} async-done(((bf16[2048,768]{1,0:T(8,128)(2,1)}), bf16[512,768]{1,0:T(8,128)(2,1)}) %reduce-scatter.7.cloned.1.call-update) | async-done | bytes 786448 | tf_op jit(solution)/shard_map/reduce_scatter | solution.py:153
  334.2 28.4 %all-gather.12.cloned.1.call-done = bf16[2048,768]{1,0:T(8,128)(2,1)} async-done(((bf16[512,768]{1,0:T(8,128)(2,1)}), bf16[2048,768]{1,0:T(8,128)(2,1)}) %all-gather.12.cloned.1.call-update) | async-done | bytes 3145744 | tf_op jit(solution)/shard_map/all_gather | solution.py:162
  362.7 9.0 %fusion.9 = bf16[2048,768]{1,0:T(8,128)(2,1)S(1)} fusion(f32[2048,768]{1,0:T(8,128)} %copy-done.168, bf16[2048,768]{1,0:T(8,128)(2,1)} %all-gather.12.cloned.1.call-done, bf16[768,1536]{0,1:T(8,128)(2,1)} %constant_dynamic-update-slice_fusion, s32[]{:T(128)S(6)} %select_n.25), kind=kOutput, calls=%fused_computation.11 | convolution fusion | flops 2447376384 | bytes 13762564 | tf_op jit(solution)/shard_map/nd,fd->nf/dot_general | solution.py:164
  373.4 4.1 convolution_convert_fusion
  377.5 38.0 %reduce-scatter.9.cloned.1.call-done = bf16[512,768]{1,0:T(8,128)(2,1)} async-done(((bf16[2048,768]{1,0:T(8,128)(2,1)}), bf16[512,768]{1,0:T(8,128)(2,1)}) %reduce-scatter.9.cloned.1.call-update) | async-done | bytes 786448 | tf_op jit(solution)/shard_map/reduce_scatter | solution.py:167
  415.5 3.2 multiply_reduce_fusion.1
  424.8 8.4 %convolution_convert_fusion.2 = bf16[768,768]{0,1:T(8,128)(2,1)} fusion(bf16[2048,768]{1,0:T(8,128)(2,1)} %all-gather.12.cloned.1.call-done, f32[2048,768]{1,0:T(8,128)} %copy-done.168), kind=kOutput, calls=%fused_computation.133 | convolution fusion | flops 2430664704 | bytes 10616832 | tf_op jit(solution)/shard_map/nf,nd->fd/dot_general | solution.py:163
  433.2 5.5 all-to-all-start.3
  439.4 9.9 %all-gather.14.cloned.1.call-done = bf16[2048,768]{1,0:T(8,128)(2,1)} async-done(((bf16[512,768]{1,0:T(8,128)(2,1)}), bf16[2048,768]{1,0:T(8,128)(2,1)}) %all-gather.14.cloned.1.call-update) | async-done | bytes 3145744 | tf_op jit(solution)/shard_map/all_gather | solution.py:177
  449.3 3.1 fusion.220
  452.5 8.0 %multiply_reduce_fusion.34 = (f32[3]{0:T(128)S(1)}, f32[3]{0:T(128)S(1)}, f32[3]{0:T(128)S(1)}, f32[3]{0:T(128)S(1)}, f32[3]{0:T(128)S(1)}, /*index=5*/f32[3]{0:...) fusion(f32[3,2048,64]{1,2,0:T(8,128)S(1)} %bitcast.248, ...), kind=kLoop, calls=%fused_computation.117 | loop fusion | flops 14155722 | bytes 3145944 | tf_op jit(solution)/shard_map/transpose(jvp())/reduce_sum | solution.py:64
  476.0 7.8 %multiply_reduce_fusion.33 = (f32[3]{0:T(128)S(1)}, f32[3]{0:T(128)S(1)}, f32[3]{0:T(128)S(1)}, f32[3]{0:T(128)S(1)}, f32[3]{0:T(128)S(1)}, /*index=5*/f32[3]{0:...) fusion(f32[3,2048,64]{1,2,0:T(8,128)S(1)} %bitcast.250, ...), kind=kLoop, calls=%fused_computation.116 | loop fusion | flops 12976083 | bytes 7864536 | tf_op jit(solution)/shard_map/transpose(jvp())/reduce_sum | solution.py:64
  490.9 40.4 %all-reduce.67 = (f32[12]{0:T(128)S(1)}, f32[12,33]{1,0:T(8,128)}, f32[4,768]{1,0:T(4,128)}) all-reduce(f32[12]{0:T(128)S(1)} %fusion.173, f32[12,33]{1,0:T(8,128)S(1)} %dynamic_update_slice.7, f32[4,768]{1,0:T(4,128)} %pad_maximum_fusion.3), channel_id=1, replica_groups=mesh['fsdp'=8,'tensor'=4] {'fsdp','tensor'}, use_global_device_ids=true, to_apply=%region_26.27 | all-reduce | flops 3480 | bytes 27840 | tf_op jit(solution)/shard_map/psum | solution.py:193
  536.5 7.4 %broadcast_multiply_fusion.1 = (f32[3,2048,64]{1,2,0:T(8,128)}, f32[3,2048,64]{1,2,0:T(8,128)}, f32[3,2048,64]{1,2,0:T(8,128)}, f32[3,2048,64]{1,2,0:T(8,128)}, ...) fusion(f32[3,2048,64]{1,2,0:T(8,128)S(1)} %bitcast.251, ...), kind=kLoop, calls=%fused_computation.219 | loop fusion | flops 4718592 | bytes 20447376 | tf_op jit(solution)/shard_map/transpose(jvp())/mul | solution.py:64
  544.1 11.1 %broadcast_multiply_fusion = (f32[3,2048,64]{1,2,0:T(8,128)}, f32[3,2048,64]{1,2,0:T(8,128)}, f32[3,2048,64]{1,2,0:T(8,128)}, f32[3,2048,64]{1,2,0:T(8,128)}, f3...) fusion(f32[3,2048,64]{1,2,0:T(8,128)S(1)} %bitcast.252, ...), kind=kLoop, calls=%fused_computation.218 | loop fusion | flops 7077888 | bytes 29884632 | tf_op jit(solution)/shard_map/transpose(jvp())/mul | solution.py:64
  573.6 5.7 fusion.54
  579.3 2.9 fusion.55
  582.2 18.5 %pad_add_fusion = f32[3,2080,64]{1,2,0:T(8,128)S(1)} fusion(f32[3,2048,64]{1,2,0:T(8,128)S(1)} %copy-done.11, f32[3,2048,64]{1,2,0:T(8,128)S(1)} %copy-done.12, f32[3,2048,64]{1,2,0:T(8,128)S(1)} %copy-done.13, f32[3,2048,64]{1,2,0:T(8,128)} %get-tuple-element.129, f32[3,2048,64]{1,2,0:T(8,128)} %get-tuple-element.130, ...), kind=kLoop, calls=%fused_computation.74 | loop fusion | flops 10383360 | bytes 44064768 | tf_op jit(solution)/shard_map/transpose(jvp())/add_any | solution.py:64
  600.8 7.5 %fusion.53 = bf16[3,2048,64]{1,2,0:T(8,128)(2,1)S(1)} fusion(f32[3,64,64]{2,1,0:T(8,128)S(1)} %copy-done.51, f32[3,2048,64]{1,2,0:T(8,128)} %get-tuple-element.119, f32[3,2048,64]{1,2,0:T(8,128)} %get-tuple-element.120, f32[3,2048,64]{1,2,0:T(8,128)} %get-tuple-element.121, f32[3,2048,64]{1,2,0:T(8,128)} %get-tuple-element.123, ...), kind=kOutput, calls=%fused_computation.66 | convolution fusion | flops 305528832 | bytes 13419264 | tf_op jit(solution)/shard_map/transpose(jvp(hin,hnd->hid))/dot_general | solution.py:58
  609.2 4.1 bitcast_convert_fusion
  613.4 6.7 convolution_convert_fusion.3
  620.1 5.3 all-to-all-start.2
  628.6 25.1 %all-to-all-done.2 = bf16[8,96,768]{2,1,0:T(8,128)(2,1)} async-done(((bf16[8,96,768]{2,1,0:T(8,128)(2,1)}), bf16[8,96,768]{2,1,0:T(8,128)(2,1)}, u32[]{:S(2)}, u32[]{:S(2)}) %all-to-all-start.2) | async-done | bytes 1179680 | tf_op jit(solution)/shard_map/all_to_all | solution.py:19
  653.7 3.5 all-to-all-start.1
  657.2 4.4 fusion.61
  664.1 5.0 all-to-all-done.1
  669.1 3.6 all-to-all-start
  678.4 23.0 %all-to-all-done = bf16[8,3,96,192]{2,3,1,0:T(8,128)(2,1)S(1)} async-done(((bf16[8,3,96,192]{2,3,1,0:T(8,128)(2,1)}), bf16[8,3,96,192]{2,3,1,0:T(8,128)(2,1)S(1)}, u32[]{:S(2)}, u32[]{:S(2)}) %all-to-all-start) | async-done | bytes 884768 | tf_op jit(solution)/shard_map/all_to_all | solution.py:19
  (543 shorter events, 133.0 us)
Async XLA Ops:
  8.0 78.3 %all-gather.6.cloned.1.call-start = ((), (), s32[]{:S(2)}) async-start(), calls=%async_computation.8 | async-start | bytes 3932160 | tf_op jit(solution)/shard_map/all_gather | solution.py:107
  10.5 209.7 %reduce-scatter.5.cloned.1.call-start = ((), (), s32[]{:S(2)}) async-start(), calls=%async_computation.9 | async-start | bytes 7864320 | tf_op jit(solution)/shard_map/reduce_scatter | solution.py:142
  93.9 10.0 %copy-start.2 = (f32[1,2048,192]{1,2,0:T(8,128)}, f32[1,2048,192]{1,2,0:T(8,128)S(1)}, u32[]{:S(2)}) copy-start(f32[1,2048,192]{1,2,0:T(8,128)S(1)} %get-tuple-element.116) | copy-start | bytes 4718596
  145.0 15.1 %copy-start.91 = (f32[3,64,64]{2,1,0:T(8,128)}, f32[3,64,64]{2,1,0:T(8,128)S(1)}, u32[]{:S(2)}) copy-start(f32[3,64,64]{2,1,0:T(8,128)S(1)} %fusion.217) | copy-start | bytes 147460
  145.7 14.4 %copy-start.21 = (bf16[192,768]{0,1:T(8,128)(2,1)S(1)}, bf16[192,768]{0,1:T(8,128)(2,1)}, u32[]{:S(2)}) copy-start(bf16[192,768]{0,1:T(8,128)(2,1)} %all_gather.23) | copy-start | bytes 884740
  163.9 115.0 %all-gather.10.cloned.1.call-start = ((), (), s32[]{:S(2)}) async-start(), calls=%async_computation.11 | async-start | bytes 1327104 | tf_op jit(solution)/shard_map/all_gather | solution.py:125
  164.5 114.4 %all-gather.8.cloned.1.call-start = ((), (), s32[]{:S(2)}) async-start(), calls=%async_computation.10 | async-start | bytes 3932160 | tf_op jit(solution)/shard_map/all_gather | solution.py:149
  224.3 102.9 %reduce-scatter.7.cloned.1.call-start = ((), (), s32[]{:S(2)}) async-start(), calls=%async_computation.12 | async-start | bytes 3932160 | tf_op jit(solution)/shard_map/reduce_scatter | solution.py:153
  224.3 8.4 %collective-permute-start = (bf16[768,96]{0,1:T(8,128)(2,1)}, bf16[768,96]{0,1:T(8,128)(2,1)S(1)}, u32[]{:S(2)}, u32[]{:S(2)}) collective-permute-start(bf16[768,96]{0,1:T(8,128)(2,1)} %param.16), channel_id=1, source_target_pairs={{0,4},{4,8},{8,12},{12,16},{16,20},{20,24},{24,28},{28,0},{1,5},{5... | collective-permute-start | bytes 442376 | tf_op jit(solution)/shard_map/ppermute | solution.py:116
  233.4 7.9 %collective-permute-start.1 = (bf16[768,96]{0,1:T(8,128)(2,1)S(1)}, bf16[768,96]{0,1:T(8,128)(2,1)S(1)}, u32[]{:S(2)}, u32[]{:S(2)}) collective-permute-start(bf16[768,96]{0,1:T(8,128)(2,1)S(1)} %collective-permute-done), channel_id=1, source_target_pairs={{0,4},{4,8},{8,12},{12,16},{16,20},{20,24},{24,28},{28,0},{1,5},{5... | collective-permute-start | bytes 442376 | tf_op jit(solution)/shard_map/ppermute | solution.py:116
  233.4 8.8 %collective-permute-start.4 = (bf16[768,96]{0,1:T(8,128)(2,1)}, bf16[768,96]{0,1:T(8,128)(2,1)}, u32[]{:S(2)}, u32[]{:S(2)}) collective-permute-start(bf16[768,96]{0,1:T(8,128)(2,1)} %param.16), channel_id=1, source_target_pairs={{0,28},{4,0},{8,4},{12,8},{16,12},{20,16},{24,20},{28,24},{1,29},{... | collective-permute-start | bytes 442376 | tf_op jit(solution)/shard_map/ppermute | solution.py:118
  242.0 8.0 %collective-permute-start.2 = (bf16[768,96]{0,1:T(8,128)(2,1)S(1)}, bf16[768,96]{0,1:T(8,128)(2,1)}, u32[]{:S(2)}, u32[]{:S(2)}) collective-permute-start(bf16[768,96]{0,1:T(8,128)(2,1)S(1)} %collective-permute-done.1), channel_id=1, source_target_pairs={{0,4},{4,8},{8,12},{12,16},{16,20},{20,24},{24,28},{28,0},{1,5},{5... | collective-permute-start | bytes 442376 | tf_op jit(solution)/shard_map/ppermute | solution.py:116
  242.1 7.8 %collective-permute-start.5 = (bf16[768,96]{0,1:T(8,128)(2,1)}, bf16[768,96]{0,1:T(8,128)(2,1)}, u32[]{:S(2)}, u32[]{:S(2)}) collective-permute-start(bf16[768,96]{0,1:T(8,128)(2,1)} %collective-permute-done.4), channel_id=1, source_target_pairs={{0,28},{4,0},{8,4},{12,8},{16,12},{20,16},{24,20},{28,24},{1,29},{... | collective-permute-start | bytes 442376 | tf_op jit(solution)/shard_map/ppermute | solution.py:118
  250.0 8.2 %collective-permute-start.3 = (bf16[768,96]{0,1:T(8,128)(2,1)}, bf16[768,96]{0,1:T(8,128)(2,1)}, u32[]{:S(2)}, u32[]{:S(2)}) collective-permute-start(bf16[768,96]{0,1:T(8,128)(2,1)} %collective-permute-done.2), channel_id=1, source_target_pairs={{0,4},{4,8},{8,12},{12,16},{16,20},{20,24},{24,28},{28,0},{1,5},{5... | collective-permute-start | bytes 442376 | tf_op jit(solution)/shard_map/ppermute | solution.py:116
  250.0 23.1 %copy-start.83 = (bf16[768,96]{0,1:T(8,128)(2,1)S(1)}, bf16[768,96]{0,1:T(8,128)(2,1)}, u32[]{:S(2)}) copy-start(bf16[768,96]{0,1:T(8,128)(2,1)} %copy-done.82) | copy-start | bytes 442372
  250.0 23.8 %copy-start.81 = (bf16[768,96]{0,1:T(8,128)(2,1)S(1)}, bf16[768,96]{0,1:T(8,128)(2,1)}, u32[]{:S(2)}) copy-start(bf16[768,96]{0,1:T(8,128)(2,1)} %copy-done.80) | copy-start | bytes 442372
  250.0 19.3 %collective-permute-start.6 = (bf16[768,96]{0,1:T(8,128)(2,1)}, bf16[768,96]{0,1:T(8,128)(2,1)S(1)}, u32[]{:S(2)}, u32[]{:S(2)}) collective-permute-start(bf16[768,96]{0,1:T(8,128)(2,1)} %collective-permute-done.5), channel_id=1, source_target_pairs={{0,28},{4,0},{8,4},{12,8},{16,12},{20,16},{24,20},{28,24},{1,29},{... | collective-permute-start | bytes 442376 | tf_op jit(solution)/shard_map/ppermute | solution.py:118
  259.7 14.7 %copy-start.79 = (bf16[768,96]{0,1:T(8,128)(2,1)S(1)}, bf16[768,96]{0,1:T(8,128)(2,1)}, u32[]{:S(2)}) copy-start(bf16[768,96]{0,1:T(8,128)(2,1)} %param.16) | copy-start | bytes 442372
  293.1 69.6 %all-gather.12.cloned.1.call-start = ((), (), s32[]{:S(2)}) async-start(), calls=%async_computation.13 | async-start | bytes 3932160 | tf_op jit(solution)/shard_map/all_gather | solution.py:162
  334.2 81.3 %reduce-scatter.9.cloned.1.call-start = ((), (), s32[]{:S(2)}) async-start(), calls=%async_computation.14 | async-start | bytes 3932160 | tf_op jit(solution)/shard_map/reduce_scatter | solution.py:167
  362.7 10.7 %copy-start.162 = (bf16[768,768]{1,0:T(8,128)(2,1)S(1)}, bf16[768,768]{1,0:T(8,128)(2,1)}, u32[]{:S(2)}) copy-start(bf16[768,768]{1,0:T(8,128)(2,1)} %all-gather.10.cloned.1.call-done) | copy-start | bytes 3538948
  377.5 71.9 %all-gather.14.cloned.1.call-start = ((), (), s32[]{:S(2)}) async-start(), calls=%async_computation.15 | async-start | bytes 3932160 | tf_op jit(solution)/shard_map/all_gather | solution.py:177
  433.2 186.9 %all-to-all-start.3 = ((bf16[8,768,96]{1,2,0:T(8,128)(2,1)}), bf16[8,768,96]{1,2,0:T(8,128)(2,1)}, u32[]{:S(2)}, u32[]{:S(2)}) async-start(bf16[8,768,96]{1,2,0:T(8,128)(2,1)} %bitcast.70), calls=%async_computation.7 | async-start | bytes 2359296 | tf_op jit(solution)/shard_map/all_to_all | solution.py:19
  438.7 263.8 %reduce-scatter.11.cloned.1.call-start = ((), (), s32[]{:S(2)}) async-start(), calls=%async_computation.16 | async-start | bytes 3932160 | tf_op jit(solution)/shard_map/reduce_scatter | solution.py:210
  452.5 8.0 %copy-start.16 = (f32[3,2048,64]{1,2,0:T(8,128)S(1)}, f32[3,2048,64]{1,2,0:T(8,128)}, u32[]{:S(2)}) copy-start(f32[3,2048,64]{1,2,0:T(8,128)} %copy-done.15) | copy-start | bytes 4718596
  484.1 47.2 %copy-start.105 = (f32[3]{0:T(128)S(1)}, f32[3]{0:T(128)}, u32[]{:S(2)}) copy-start(f32[3]{0:T(128)} %copy-done.103) | copy-start | bytes 40
  484.7 49.4 %copy-start.34 = (f32[3,64,64]{2,1,0:T(8,128)S(1)}, f32[3,64,64]{2,1,0:T(8,128)}, u32[]{:S(2)}) copy-start(f32[3,64,64]{2,1,0:T(8,128)} %copy-done.33) | copy-start | bytes 147460
  490.8 66.1 %copy-start.50 = (f32[3,64,64]{2,1,0:T(8,128)}, f32[3,64,64]{2,1,0:T(8,128)S(1)}, u32[]{:S(2)}) copy-start(f32[3,64,64]{2,1,0:T(8,128)S(1)} %fusion.221) | copy-start | bytes 147460
  536.4 7.5 %copy-start.108 = (f32[3]{0:T(128)S(1)}, f32[3]{0:T(128)}, u32[]{:S(2)}) copy-start(f32[3]{0:T(128)} %get-tuple-element.89) | copy-start | bytes 40
  536.4 7.5 %copy-start.110 = (f32[3]{0:T(128)S(1)}, f32[3]{0:T(128)}, u32[]{:S(2)}) copy-start(f32[3]{0:T(128)} %get-tuple-element.90) | copy-start | bytes 40
  536.4 7.5 %copy-start.112 = (f32[3]{0:T(128)S(1)}, f32[3]{0:T(128)}, u32[]{:S(2)}) copy-start(f32[3]{0:T(128)} %get-tuple-element.91) | copy-start | bytes 40
  536.4 7.5 %copy-start.114 = (f32[3]{0:T(128)S(1)}, f32[3]{0:T(128)}, u32[]{:S(2)}) copy-start(f32[3]{0:T(128)} %get-tuple-element.92) | copy-start | bytes 40
  536.4 7.5 %copy-start.116 = (f32[3]{0:T(128)S(1)}, f32[3]{0:T(128)}, u32[]{:S(2)}) copy-start(f32[3]{0:T(128)} %get-tuple-element.93) | copy-start | bytes 40
  536.4 7.5 %copy-start.118 = (f32[3]{0:T(128)S(1)}, f32[3]{0:T(128)}, u32[]{:S(2)}) copy-start(f32[3]{0:T(128)} %get-tuple-element.94) | copy-start | bytes 40
  536.4 7.5 %copy-start.120 = (f32[3]{0:T(128)S(1)}, f32[3]{0:T(128)}, u32[]{:S(2)}) copy-start(f32[3]{0:T(128)} %get-tuple-element.95) | copy-start | bytes 40
  536.4 7.5 %copy-start.122 = (f32[3]{0:T(128)S(1)}, f32[3]{0:T(128)}, u32[]{:S(2)}) copy-start(f32[3]{0:T(128)} %get-tuple-element.96) | copy-start | bytes 40
  544.1 11.1 %copy-start.17 = (f32[3,2048,64]{1,2,0:T(8,128)S(1)}, f32[3,2048,64]{1,2,0:T(8,128)}, u32[]{:S(2)}) copy-start(f32[3,2048,64]{1,2,0:T(8,128)} %copy-done.15) | copy-start | bytes 4718596
  544.1 11.1 %copy-start.92 = (f32[3,64,64]{2,1,0:T(8,128)S(1)}, f32[3,64,64]{2,1,0:T(8,128)}, u32[]{:S(2)}) copy-start(f32[3,64,64]{2,1,0:T(8,128)} %copy-done.91) | copy-start | bytes 147460
  582.2 18.5 %copy-start.51 = (f32[3,64,64]{2,1,0:T(8,128)S(1)}, f32[3,64,64]{2,1,0:T(8,128)}, u32[]{:S(2)}) copy-start(f32[3,64,64]{2,1,0:T(8,128)} %copy-done.50) | copy-start | bytes 147460
  600.7 8.5 %copy-start.32 = (bf16[3,768,192]{2,0,1:T(4,128)(2,1)S(1)}, bf16[3,768,192]{2,0,1:T(4,128)(2,1)}, u32[]{:S(2)}) copy-start(bf16[3,768,192]{2,0,1:T(4,128)(2,1)} %copy-done.31) | copy-start | bytes 2654212
  600.8 8.4 %copy-start.163 = (bf16[3,2048,64]{1,2,0:T(8,128)(2,1)S(1)}, bf16[3,2048,64]{1,2,0:T(8,128)(2,1)}, u32[]{:S(2)}) copy-start(bf16[3,2048,64]{1,2,0:T(8,128)(2,1)} %fusion.54) | copy-start | bytes 2359300
  600.8 8.4 %copy-start.164 = (bf16[3,2048,64]{1,2,0:T(8,128)(2,1)S(1)}, bf16[3,2048,64]{1,2,0:T(8,128)(2,1)}, u32[]{:S(2)}) copy-start(bf16[3,2048,64]{1,2,0:T(8,128)(2,1)} %fusion.55) | copy-start | bytes 2359300
  613.4 12.0 %copy-start.9 = (bf16[2048,768]{1,0:T(8,128)(2,1)S(1)}, bf16[2048,768]{1,0:T(8,128)(2,1)}, u32[]{:S(2)}) copy-start(bf16[2048,768]{1,0:T(8,128)(2,1)} %all-gather.14.cloned.1.call-done) | copy-start | bytes 9437188
  620.1 33.7 %all-to-all-start.2 = ((bf16[8,96,768]{2,1,0:T(8,128)(2,1)}), bf16[8,96,768]{2,1,0:T(8,128)(2,1)}, u32[]{:S(2)}, u32[]{:S(2)}) async-start(bf16[8,96,768]{2,1,0:T(8,128)(2,1)} %bitcast.271), calls=%async_computation.6 | async-start | bytes 2359296 | tf_op jit(solution)/shard_map/all_to_all | solution.py:19
  627.3 29.9 %copy-start.78 = (bf16[3,2048,64]{1,2,0:T(8,128)(2,1)S(1)}, bf16[3,2048,64]{1,2,0:T(8,128)(2,1)}, u32[]{:S(2)}) copy-start(bf16[3,2048,64]{1,2,0:T(8,128)(2,1)} %copy-done.77) | copy-start | bytes 2359300
  653.7 15.4 %all-to-all-start.1 = ((bf16[8,192,96]{2,1,0:T(8,128)(2,1)}), bf16[8,192,96]{2,1,0:T(8,128)(2,1)S(1)}, u32[]{:S(2)}, u32[]{:S(2)}) async-start(bf16[8,192,96]{2,1,0:T(8,128)(2,1)} %bitcast.247), calls=%async_computation.5 | async-start | bytes 786432 | tf_op jit(solution)/shard_map/all_to_all | solution.py:19
  669.1 32.3 %all-to-all-start = ((bf16[8,3,96,192]{2,3,1,0:T(8,128)(2,1)}), bf16[8,3,96,192]{2,3,1,0:T(8,128)(2,1)S(1)}, u32[]{:S(2)}, u32[]{:S(2)}) async-start(bf16[8,3,96,192]{2,3,1,0:T(8,128)(2,1)} %bitcast.246), calls=%async_computation.4 | async-start | bytes 2359296 | tf_op jit(solution)/shard_map/all_to_all | solution.py:19
  677.1 25.5 %copy-start.19 = (f32[512,768]{1,0:T(8,128)S(1)}, f32[512,768]{1,0:T(8,128)}, u32[]{:S(2)}) copy-start(f32[512,768]{1,0:T(8,128)} %get-tuple-element.108) | copy-start | bytes 4718596
  (141 other events, 405.5 us)
Sparse Core Ops, SparseCore 0:
  11.0 31.2 all-gather.5
  164.1 56.1 reduce-scatter.4
  377.6 37.8 reduce-scatter.8
Sparse Core Ops, SparseCore 1:
  166.6 38.6 all-gather.9
  224.4 28.3 all-gather.7
  293.2 34.0 reduce-scatter.6
  334.3 28.3 all-gather.11
  420.9 28.3 all-gather.13
  613.5 38.8 reduce-scatter.10
